TPU v7x, 32 devices: a whole 2x2x4 slice. The times are simulated.
32 devices in a mesh: src: 8 (over z, x), tgt: 4 (over y, core).
Axes of the slice: x: 2, y: 2, z: 4, core: 2. Of those that a mesh axis runs over, the one named last changes fastest.
Arguments:
- source_words: bfloat16 [4096, 300], P(('src', 'tgt')), may hold values from -3 to 3
- target_words: bfloat16 [3840, 300], P(('tgt', 'src')), may hold values from -24 to 24
Outputs:
- rotated: bfloat16 [4096, 300], P(('src', 'tgt'))
- matched: float32 [4096, 300], P(('src', 'tgt'))
- ortho: float32 [300, 300], replicated
- row_pot: float32 [4096], P(('src', 'tgt'))
- col_pot: float32 [3840], P(('tgt', 'src'))
All inputs are finite; a program needn't handle non-finite values.
Results may differ from a plain program's by a relative error of at most 0.0034.
Values may be sent and summed in bfloat16 or wider, within the bound.
No kernel may reach another device: no remote copies, remote signals or barrier semaphores. Data moves between devices by JAX's collectives and lax.ppermute only.
A program may use at most 64 MiB of HBM per device.

v0:
```python
import math
import jax
import jax.numpy as jnp
from jax import lax
from jax.sharding import PartitionSpec as P

ITERS = 2
NEWTON = 12


def reduce_rows(top, total):
    higher = lax.pmax(top, "tgt")
    whole = lax.psum(total * jnp.exp(top - higher), "tgt")
    return -(higher + jnp.log(whole))


def reduce_cols(top, total):
    higher = lax.pmax(top, "src")
    whole = lax.psum(total * jnp.exp(top - higher), "src")
    return -(higher + jnp.log(whole))


def body(source_words, target_words):
    width = source_words.shape[1]
    scale = 4.0 / math.sqrt(width)
    highest = lax.Precision.HIGHEST
    src_block = lax.all_gather(source_words, "tgt", axis=0, tiled=True)
    rows = src_block.shape[0]
    cols = target_words.shape[0] * lax.axis_size("src")
    inner = (((1,), (1,)), ((), ()))
    leading = (((0,), (0,)), ((), ()))

    def scores(piece):
        return lax.dot_general(src_block, piece, inner, preferred_element_type=jnp.float32) * scale

    col_pot = jnp.zeros((cols,), jnp.float32)
    row_pot = jnp.zeros((rows,), jnp.float32)
    for sweep_index in range(ITERS):
        row_top = jnp.full((rows,), -jnp.inf, jnp.float32)
        total = jnp.zeros((rows,), jnp.float32)
        row_shift = col_pot
        row_logits = (
            scores(lax.all_gather(target_words, "src", axis=0, tiled=True)) + row_shift[None, :]
        )
        higher = jnp.max(row_logits, axis=1)
        total = total * jnp.exp(row_top - higher) + jnp.sum(
            jnp.exp(row_logits - higher[:, None]), axis=1
        )
        top, total = (higher, total)
        row_pot = reduce_rows(top, total)
        logits = scores(lax.all_gather(target_words, "src", axis=0, tiled=True)) + row_pot[:, None]
        col_top = jnp.max(logits, axis=0)
        parts = jnp.stack([col_top, jnp.sum(jnp.exp(logits - col_top[None, :]), axis=0)])
        col_pot = reduce_cols(parts[0], parts[1])
    piece = lax.all_gather(target_words, "src", axis=0, tiled=True)
    plan = jnp.exp(scores(piece) + row_pot[:, None] + col_pot[None, :]).astype(jnp.bfloat16)
    summed = jnp.dot(plan, piece, preferred_element_type=jnp.float32)
    matched = lax.psum_scatter(summed, "tgt", scatter_dimension=0, tiled=True)
    term = lax.dot_general(source_words.astype(jnp.float32), matched, leading, precision=highest)
    cov = lax.psum(term, ("src", "tgt"))
    ortho = cov / jnp.sqrt(jnp.sum(cov * cov) + 1e-06)
    for step_index in range(NEWTON):
        ortho = 1.5 * ortho - 0.5 * jnp.dot(
            ortho, jnp.dot(ortho.T, ortho, precision=highest), precision=highest
        )
    rotated = jnp.dot(source_words.astype(jnp.float32), ortho, precision=highest).astype(
        jnp.bfloat16
    )
    own_rows = rows // lax.axis_size("tgt")
    own_cols = cols // lax.axis_size("src")
    row_part = lax.dynamic_slice_in_dim(row_pot, lax.axis_index("tgt") * own_rows, own_rows)
    col_part = lax.dynamic_slice_in_dim(col_pot, lax.axis_index("src") * own_cols, own_cols)
    return (rotated, matched, ortho, row_part, col_part)


def solution(mesh):
    in_specs = (P(("src", "tgt"), None), P(("tgt", "src"), None))
    out_specs = (
        P(("src", "tgt"), None),
        P(("src", "tgt"), None),
        P(),
        P(("src", "tgt")),
        P(("tgt", "src")),
    )
    return jax.shard_map(body, mesh=mesh, in_specs=in_specs, out_specs=out_specs, check_vma=False)
```

profile of v0, /device:TPU:0, one launch (start us, length us, event | category | flops | bytes accessed | tf_op | source)
XLA Modules:
  0.0 346.5 jit_solution(8478248790256403142)
XLA Ops:
  7.2 0.0 copy-start
  7.2 0.0 reduce-scatter.2.cloned.1.call-start
  7.2 33.5 %all-gather = bf16[8,120,300]{1,2,0:T(8,128)(2,1)S(1)} all-gather(bf16[1,120,300]{1,2,0:T(8,128)(2,1)} %bitcast.59), channel_id=1, replica_groups=mesh['src'=8,'tgt'=4] {'src'}, dimensions={0}, use_global_device_ids=true | all-gather | bytes 648000 | tf_op jit(solution)/shard_map/all_gather | solution.py:55
  40.7 0.2 copy.34
  40.9 0.5 reshape.19
  41.4 0.0 copy-done
  41.4 6.1 %all_gather.4 = bf16[512,300]{0,1:T(8,128)(2,1)S(1)} all-gather(bf16[128,300]{0,1:T(8,128)(2,1)S(1)} %copy-done), channel_id=1, replica_groups=mesh['src'=8,'tgt'=4] {'tgt'}, dimensions={0}, use_global_device_ids=true | all-gather | bytes 384000 | tf_op jit(solution)/shard_map/all_gather | solution.py:27
  47.5 0.7 fusion.17
  48.3 7.0 %pmax.28 = f32[512]{0:T(512)S(1)} all-reduce(f32[512]{0:T(512)S(1)} %get-tuple-element.20), channel_id=1, replica_groups=mesh['src'=8,'tgt'=4] {'tgt'}, use_global_device_ids=true, to_apply=%region_1.0 | all-reduce | flops 512 | bytes 4096 | tf_op jit(solution)/shard_map/pmax | solution.py:12
  55.2 0.3 exponential_reduce_fusion.3
  55.6 5.7 %psum.35 = f32[512]{0:T(512)S(1)} all-reduce(f32[512]{0:T(512)S(1)} %exponential_multiply_fusion.3), channel_id=1, replica_groups=mesh['src'=8,'tgt'=4] {'tgt'}, use_global_device_ids=true, to_apply=%region_3.0 | all-reduce | flops 512 | bytes 4096 | tf_op jit(solution)/shard_map/psum | solution.py:13
  61.3 0.2 add_reduce_fusion.1
  61.5 0.6 exponential_reduce_fusion.2
  62.0 21.5 %pmax.29 = f32[960]{0:T(1024)S(1)} all-reduce(f32[960]{0:T(1024)S(1)} %add_reduce_fusion.1), channel_id=1, replica_groups=mesh['src'=8,'tgt'=4] {'src'}, use_global_device_ids=true, to_apply=%region_5.0 | all-reduce | flops 960 | bytes 7680 | tf_op jit(solution)/shard_map/pmax | solution.py:18
  83.5 17.1 %psum.36 = f32[960]{0:T(1024)S(1)} all-reduce(f32[960]{0:T(1024)S(1)} %exponential_multiply_fusion.1), channel_id=1, replica_groups=mesh['src'=8,'tgt'=4] {'src'}, use_global_device_ids=true, to_apply=%region_7.0 | all-reduce | flops 960 | bytes 7680 | tf_op jit(solution)/shard_map/psum | solution.py:19
  100.7 0.2 add_reduce_fusion
  100.9 0.4 exponential_reduce_fusion.1
  101.3 5.7 %pmax.30 = f32[512]{0:T(512)S(1)} all-reduce(f32[512]{0:T(512)S(1)} %add_reduce_fusion), channel_id=1, replica_groups=mesh['src'=8,'tgt'=4] {'tgt'}, use_global_device_ids=true, to_apply=%region_9.0 | all-reduce | flops 512 | bytes 4096 | tf_op jit(solution)/shard_map/pmax | solution.py:12
  107.0 6.0 %psum.37 = f32[512]{0:T(512)S(1)} all-reduce(f32[512]{0:T(512)S(1)} %exponential_multiply_fusion.2), channel_id=1, replica_groups=mesh['src'=8,'tgt'=4] {'tgt'}, use_global_device_ids=true, to_apply=%region_11.0 | all-reduce | flops 512 | bytes 4096 | tf_op jit(solution)/shard_map/psum | solution.py:13
  113.0 0.2 add_reduce_fusion.2
  113.3 0.6 exponential_reduce_fusion
  113.8 19.1 %pmax.31 = f32[960]{0:T(1024)S(1)} all-reduce(f32[960]{0:T(1024)S(1)} %add_reduce_fusion.2), channel_id=1, replica_groups=mesh['src'=8,'tgt'=4] {'src'}, use_global_device_ids=true, to_apply=%region_13.0 | all-reduce | flops 960 | bytes 7680 | tf_op jit(solution)/shard_map/pmax | solution.py:18
  133.0 17.2 %psum.38 = f32[960]{0:T(1024)S(1)} all-reduce(f32[960]{0:T(1024)S(1)} %exponential_multiply_fusion), channel_id=1, replica_groups=mesh['src'=8,'tgt'=4] {'src'}, use_global_device_ids=true, to_apply=%region_15.0 | all-reduce | flops 960 | bytes 7680 | tf_op jit(solution)/shard_map/psum | solution.py:19
  150.2 1.4 fusion.13
  151.6 0.0 reduce-scatter.2.cloned.1.call-update
  151.6 0.2 all-reduce.2.cloned.1.call-start
  151.9 20.7 %reduce-scatter.2.cloned.1.call-done = f32[128,300]{0,1:T(8,128)} async-done(((f32[512,300]{0,1:T(8,128)}), f32[128,300]{0,1:T(8,128)}) %reduce-scatter.2.cloned.1.call-update) | async-done | bytes 153616 | tf_op jit(solution)/shard_map/reduce_scatter | solution.py:58
  172.5 2.0 convolution_bitcast_fusion
  174.5 0.0 all-reduce.2.cloned.1.call-update
  174.6 0.6 dynamic_slice.7
  175.2 0.6 dynamic_slice.6
  175.7 130.6 %all-reduce.2.cloned.1.call-done = f32[300,300]{0,1:T(8,128)} async-done(((f32[300,300]{0,1:T(8,128)}), f32[300,300]{0,1:T(8,128)}) %all-reduce.2.cloned.1.call-update) | async-done | bytes 360016 | tf_op jit(solution)/shard_map/psum | solution.py:60
  306.3 0.0 copy-start.1
  306.3 1.8 multiply_reduce_fusion
  308.8 2.2 fusion.16
  311.1 0.0 copy-done.1
  311.1 1.2 fusion.11
  312.3 1.0 fusion.18
  313.4 1.2 fusion.10
  314.6 1.0 fusion.19
  315.6 1.2 fusion.9
  316.8 1.0 fusion.20
  317.9 1.2 fusion.8
  319.1 1.0 fusion.21
  320.1 1.2 fusion.7
  321.4 1.3 fusion.22
  322.6 1.2 fusion.6
  323.8 1.0 fusion.23
  324.9 1.2 fusion.5
  326.1 1.0 fusion.24
  327.2 1.2 fusion.4
  328.4 1.0 fusion.25
  329.4 1.2 fusion.3
  330.6 1.0 fusion.26
  331.7 1.2 fusion.2
  332.9 1.3 fusion.27
  334.2 1.2 fusion.1
  335.4 1.0 fusion.28
  336.4 1.2 fusion
  337.7 1.0 copy.47
  338.7 1.0 fusion.12
  (8 shorter events, 0.1 us)
Async XLA Ops:
  7.2 34.2 %copy-start = (bf16[128,300]{0,1:T(8,128)(2,1)S(1)}, bf16[128,300]{0,1:T(8,128)(2,1)}, u32[]{:S(2)}) copy-start(bf16[128,300]{0,1:T(8,128)(2,1)} %param.2) | copy-start | bytes 230404
  7.2 165.4 %reduce-scatter.2.cloned.1.call-start = ((), (), s32[]{:S(2)}) async-start(), calls=%async_computation.1 | async-start | bytes 778240 | tf_op jit(solution)/shard_map/reduce_scatter | solution.py:58
  151.6 154.7 %all-reduce.2.cloned.1.call-start = ((), (), s32[]{:S(2)}) async-start(), calls=%async_computation.2 | async-start | bytes 933888 | tf_op jit(solution)/shard_map/psum | solution.py:60
  306.3 4.8 %copy-start.1 = (f32[300,300]{0,1:T(8,128)S(1)}, f32[300,300]{0,1:T(8,128)}, u32[]{:S(2)}) copy-start(f32[300,300]{0,1:T(8,128)} %all-reduce.2.cloned.1.call-done) | copy-start | bytes 1080004
Sparse Core Ops, SparseCore 0:
  151.7 20.7 reduce-scatter.1
  178.4 127.8 all-reduce.1
where the time goes:
time: 347 us; the launch traced here: 346 us
  waiting for transfers between devices  151 us (44%)
  blocking collectives  139 us (40%)
  matrix products  33.8 us (10%)
  between operations  15 us (4%)
  other arithmetic  4.41 us (1%)
    psum x1, waiting for transfers between devices, body(): cov = lax.psum(term, ('src', 'tgt'))  131 us
    pmax x2, blocking collectives, reduce_cols(): higher = lax.pmax(top, 'src')  40.6 us
    psum x2, blocking collectives, reduce_cols(): whole = lax.psum(total * jnp.exp(top - higher), 'src')  34.3 us
    all_gather x1, blocking collectives, body(): piece = lax.all_gather(target_words, 'src', axis=0, tiled=True)  33.5 us
    reduce_scatter x1, waiting for transfers between devices, body(): matched = lax.psum_scatter(summed, 'tgt', scatter_dimension=0, tiled=True)  20.7 us
    dot_general x12, matrix products, body(): jnp.dot(ortho, jnp.dot(ortho.T, ortho, precision=highest), precision=high...  14.5 us
    dot_general x12, matrix products, body(): jnp.dot(ortho.T, ortho, precision=highest)  14.1 us
    pmax x2, blocking collectives, reduce_rows(): higher = lax.pmax(top, 'tgt')  12.6 us
  transfers between devices with their start and end apart: 2, of which 2 were waited for; matrix products, arithmetic and copies ran while one was open for 0% of the time, Pallas kernels for 0%

commit v1 on v0

--- a/solution.py
+++ b/solution.py
@@ -16,7 +16,9 @@
 
 def reduce_cols(top, total):
     higher = lax.pmax(top, "src")
-    whole = lax.psum(total * jnp.exp(top - higher), "src")
+    own = total * jnp.exp(top - higher)
+    shards = lax.all_gather(own, "src", axis=0, tiled=False)
+    whole = shards.sum(axis=0)
     return -(higher + jnp.log(whole))
 
 

time: 347 us -> 379 us (1.092)
  blocking collectives: 139 us -> 170 us
    unnamed x0 -> x2, blocking collectives: none -> 67.9 us
    psum x2 -> x0, blocking collectives: 34.3 us -> none  [reduce_cols(): whole = lax.psum(total * jnp.exp(top - higher), 'src')]
where the time goes in v1:
time: 379 us; the launch traced here: 378 us
  blocking collectives  170 us (45%)
  waiting for transfers between devices  150 us (40%)
  matrix products  33.8 us (9%)
  between operations  15.7 us (4%)
  other arithmetic  4.67 us (1%)
    psum x1, waiting for transfers between devices, body(): cov = lax.psum(term, ('src', 'tgt'))  131 us
    unnamed x2, blocking collectives  67.9 us
    pmax x2, blocking collectives, reduce_cols(): higher = lax.pmax(top, 'src')  38.6 us
    all_gather x1, blocking collectives, body(): piece = lax.all_gather(target_words, 'src', axis=0, tiled=True)  33.5 us
    reduce_scatter x1, waiting for transfers between devices, body(): matched = lax.psum_scatter(summed, 'tgt', scatter_dimension=0, tiled=True)  19.3 us
    dot_general x12, matrix products, body(): jnp.dot(ortho, jnp.dot(ortho.T, ortho, precision=highest), precision=high...  14.5 us
    dot_general x12, matrix products, body(): jnp.dot(ortho.T, ortho, precision=highest)  14.1 us
    pmax x2, blocking collectives, reduce_rows(): higher = lax.pmax(top, 'tgt')  12.6 us
  transfers between devices with their start and end apart: 2, of which 2 were waited for; matrix products, arithmetic and copies ran while one was open for 0% of the time, Pallas kernels for 0%

profile of v1, /device:TPU:0, one launch (start us, length us, event | category | flops | bytes accessed | tf_op | source)
XLA Modules:
  0.0 378.4 jit_solution(6813428758265139506)
XLA Ops:
  7.2 0.0 reduce-scatter.2.cloned.1.call-start
  7.2 33.5 %all-gather.2 = bf16[8,120,300]{1,2,0:T(8,128)(2,1)S(1)} all-gather(bf16[1,120,300]{1,2,0:T(8,128)(2,1)} %bitcast.60), channel_id=1, replica_groups=mesh['src'=8,'tgt'=4] {'src'}, dimensions={0}, use_global_device_ids=true | all-gather | bytes 648000 | tf_op jit(solution)/shard_map/all_gather | solution.py:57
  40.7 0.2 copy.48
  40.9 0.5 reshape.27
  41.4 0.0 copy-done
  41.4 6.1 %all_gather.22 = bf16[512,300]{0,1:T(8,128)(2,1)S(1)} all-gather(bf16[128,300]{0,1:T(8,128)(2,1)S(1)} %copy-done), channel_id=1, replica_groups=mesh['src'=8,'tgt'=4] {'tgt'}, dimensions={0}, use_global_device_ids=true | all-gather | bytes 384000 | tf_op jit(solution)/shard_map/all_gather | solution.py:29
  47.5 0.7 fusion.17
  48.3 7.0 %pmax.28 = f32[512]{0:T(512)S(1)} all-reduce(f32[512]{0:T(512)S(1)} %get-tuple-element.25), channel_id=1, replica_groups=mesh['src'=8,'tgt'=4] {'tgt'}, use_global_device_ids=true, to_apply=%region_1.0 | all-reduce | flops 512 | bytes 4096 | tf_op jit(solution)/shard_map/pmax | solution.py:12
  55.2 0.3 exponential_reduce_fusion.3
  55.6 5.7 %psum.21 = f32[512]{0:T(512)S(1)} all-reduce(f32[512]{0:T(512)S(1)} %exponential_multiply_fusion.1), channel_id=1, replica_groups=mesh['src'=8,'tgt'=4] {'tgt'}, use_global_device_ids=true, to_apply=%region_3.0 | all-reduce | flops 512 | bytes 4096 | tf_op jit(solution)/shard_map/psum | solution.py:13
  61.3 0.2 add_reduce_fusion.1
  61.5 0.6 exponential_reduce_fusion.2
  62.0 21.5 %pmax.29 = f32[960]{0:T(1024)S(1)} all-reduce(f32[960]{0:T(1024)S(1)} %add_reduce_fusion.1), channel_id=1, replica_groups=mesh['src'=8,'tgt'=4] {'src'}, use_global_device_ids=true, to_apply=%region_5.0 | all-reduce | flops 960 | bytes 7680 | tf_op jit(solution)/shard_map/pmax | solution.py:18
  83.5 0.0 copy-done.2
  83.5 0.6 dynamic-slice
  84.8 0.1 multiply_dynamic-update-slice_fusion.1
  84.9 33.0 %all-reduce = f32[7680]{0:T(1024)S(1)} all-reduce(f32[7680]{0:T(1024)S(1)} %multiply_dynamic-update-slice_fusion.1), channel_id=2, replica_groups=mesh['src'=8,'tgt'=4] {'src'}, use_global_device_ids=true, to_apply=%add | all-reduce | flops 7680 | bytes 61440
  117.9 0.1 reshape.18
  118.0 0.2 add_reduce_fusion
  118.2 0.4 exponential_reduce_fusion.1
  118.6 5.7 %pmax.30 = f32[512]{0:T(512)S(1)} all-reduce(f32[512]{0:T(512)S(1)} %add_reduce_fusion), channel_id=1, replica_groups=mesh['src'=8,'tgt'=4] {'tgt'}, use_global_device_ids=true, to_apply=%region_9.0 | all-reduce | flops 512 | bytes 4096 | tf_op jit(solution)/shard_map/pmax | solution.py:12
  124.3 6.0 %psum.22 = f32[512]{0:T(512)S(1)} all-reduce(f32[512]{0:T(512)S(1)} %exponential_multiply_fusion), channel_id=1, replica_groups=mesh['src'=8,'tgt'=4] {'tgt'}, use_global_device_ids=true, to_apply=%region_11.0 | all-reduce | flops 512 | bytes 4096 | tf_op jit(solution)/shard_map/psum | solution.py:13
  130.4 0.2 add_reduce_fusion.2
  130.6 0.6 exponential_reduce_fusion
  131.2 17.1 %pmax.31 = f32[960]{0:T(1024)S(1)} all-reduce(f32[960]{0:T(1024)S(1)} %add_reduce_fusion.2), channel_id=1, replica_groups=mesh['src'=8,'tgt'=4] {'src'}, use_global_device_ids=true, to_apply=%region_13.0 | all-reduce | flops 960 | bytes 7680 | tf_op jit(solution)/shard_map/pmax | solution.py:18
  148.3 0.1 multiply_dynamic-update-slice_fusion
  148.4 34.9 %all-reduce.1 = f32[7680]{0:T(1024)S(1)} all-reduce(f32[7680]{0:T(1024)S(1)} %multiply_dynamic-update-slice_fusion), channel_id=3, replica_groups=mesh['src'=8,'tgt'=4] {'src'}, use_global_device_ids=true, to_apply=%add.1 | all-reduce | flops 7680 | bytes 61440
  183.3 0.1 reshape.19
  183.4 1.4 fusion.13
  184.8 0.0 reduce-scatter.2.cloned.1.call-update
  184.9 0.2 all-reduce.4.cloned.1.call-start
  185.1 19.3 %reduce-scatter.2.cloned.1.call-done = f32[128,300]{0,1:T(8,128)} async-done(((f32[512,300]{0,1:T(8,128)}), f32[128,300]{0,1:T(8,128)}) %reduce-scatter.2.cloned.1.call-update) | async-done | bytes 153616 | tf_op jit(solution)/shard_map/reduce_scatter | solution.py:60
  204.4 2.0 convolution_bitcast_fusion
  206.4 0.0 all-reduce.4.cloned.1.call-update
  206.4 0.6 dynamic_slice.7
  207.0 0.6 dynamic_slice.6
  207.6 130.7 %all-reduce.4.cloned.1.call-done = f32[300,300]{0,1:T(8,128)} async-done(((f32[300,300]{0,1:T(8,128)}), f32[300,300]{0,1:T(8,128)}) %all-reduce.4.cloned.1.call-update) | async-done | bytes 360016 | tf_op jit(solution)/shard_map/psum | solution.py:62
  338.2 1.8 multiply_reduce_fusion
  340.7 2.2 fusion.16
  343.0 1.2 fusion.11
  344.2 1.0 fusion.18
  345.3 1.2 fusion.10
  346.5 1.0 fusion.19
  347.5 1.2 fusion.9
  348.7 1.0 fusion.20
  349.8 1.2 fusion.8
  351.0 1.0 fusion.21
  352.0 1.2 fusion.7
  353.3 1.3 fusion.22
  354.5 1.2 fusion.6
  355.7 1.0 fusion.23
  356.8 1.2 fusion.5
  358.0 1.0 fusion.24
  359.1 1.2 fusion.4
  360.3 1.0 fusion.25
  361.3 1.2 fusion.3
  362.5 1.0 fusion.26
  363.6 1.2 fusion.2
  364.8 1.3 fusion.27
  366.1 1.2 fusion.1
  367.3 1.0 fusion.28
  368.3 1.2 fusion
  369.6 1.0 copy.61
  370.6 1.0 fusion.12
  (14 shorter events, 0.1 us)
Async XLA Ops:
  7.2 34.2 %copy-start = (bf16[128,300]{0,1:T(8,128)(2,1)S(1)}, bf16[128,300]{0,1:T(8,128)(2,1)}, u32[]{:S(2)}) copy-start(bf16[128,300]{0,1:T(8,128)(2,1)} %param.2) | copy-start | bytes 230404
  7.2 197.2 %reduce-scatter.2.cloned.1.call-start = ((), (), s32[]{:S(2)}) async-start(), calls=%async_computation.1 | async-start | bytes 778240 | tf_op jit(solution)/shard_map/reduce_scatter | solution.py:60
  61.3 22.3 %copy-start.2 = (u32[32]{0:T(128)S(1)}, u32[32]{0:T(128)}, u32[]{:S(2)}) copy-start(u32[32]{0:T(128)} %constant.36) | copy-start | bytes 388
  184.9 153.4 %all-reduce.4.cloned.1.call-start = ((), (), s32[]{:S(2)}) async-start(), calls=%async_computation.2 | async-start | bytes 933888 | tf_op jit(solution)/shard_map/psum | solution.py:62
  338.2 4.8 %copy-start.1 = (f32[300,300]{0,1:T(8,128)S(1)}, f32[300,300]{0,1:T(8,128)}, u32[]{:S(2)}) copy-start(f32[300,300]{0,1:T(8,128)} %all-reduce.4.cloned.1.call-done) | copy-start | bytes 1080004
Sparse Core Ops, SparseCore 0:
  185.0 19.3 reduce-scatter.1
  210.2 127.9 all-reduce.3
